TPU v7x, 32 devices: a whole 2x2x4 slice. The times are simulated.
32 devices in a mesh: gx: 8 (over z, x), gy: 4 (over y, core).
Axes of the slice: x: 2, y: 2, z: 4, core: 2. Of those that a mesh axis runs over, the one named last changes fastest.
Arguments:
- starting_thermal_values: float32 [64, 512, 128], P('gx', 'gy'), may hold values from -6 to 6
- horizontal_boundary_transmission: float32 [64, 512], P('gx', 'gy'), may hold values from 0.5 to 4
- lateral_boundary_transmission: float32 [64, 512], P('gx', 'gy'), may hold values from 0.5 to 4
- zaxis_interface_weight: float32 [64, 512], P('gx', 'gy'), may hold values from 0.5 to 4
Outputs:
- updated: float32 [64, 512, 128], P('gx', 'gy')
All inputs are finite; a program needn't handle non-finite values.
Results may differ from a plain program's by a relative error of at most 0.0045.
Values sent between devices are 32-bit elements; how exact they have to be, the bound alone decides.
A program may use at most 64 MiB of HBM per device.

v0:
```python
import jax
import jax.numpy as jnp
from jax import lax
from jax.sharding import PartitionSpec as P

leading_speed = 40000.0
trailing_speed = 40000.0
third_rate = 0.25


def with_halo(array, sides, width):
    for axis, dim in sides:
        size, length = (lax.axis_size(axis), array.shape[dim])
        up = [(i, (i + 1) % size) for i in range(size - 1)]
        down = [(j, i) for i, j in up]
        last = lax.slice_in_dim(array, length - width, length, axis=dim)
        initial = lax.slice_in_dim(array, 0, width, axis=dim)
        before = lax.ppermute(last, axis, up)
        after = lax.ppermute(initial, axis, down)
        array = jnp.concatenate([before, array, after], axis=dim)
    return array


def passed_along(block, axis, distance):
    devices = range(lax.axis_size(axis))
    route = [(i - distance, i) for i in devices if i - distance in devices]
    return lax.ppermute(block, axis, route)


def from_before(values, stride, line_dim, filler):
    length = values.shape[line_dim]
    pad_shape = list(values.shape)
    pad_shape[line_dim] = stride
    padding = jnp.full(pad_shape, filler, values.dtype)
    retained = lax.slice_in_dim(values, 0, length - stride, axis=line_dim)
    return jnp.concatenate([padding, retained], line_dim)


def from_after(values, stride, line_dim, filler):
    length = values.shape[line_dim]
    pad_shape = list(values.shape)
    pad_shape[line_dim] = stride
    padding = jnp.full(pad_shape, filler, values.dtype)
    retained = lax.slice_in_dim(values, stride, length, axis=line_dim)
    return jnp.concatenate([retained, padding], line_dim)


def reduce_lines(lower, middle, upper, vectors, line_dim):
    length = middle.shape[line_dim]
    stride = 1
    while stride < length:
        alpha_weight = -lower / from_before(middle, stride, line_dim, 1.0)
        beta_weight = -upper / from_after(middle, stride, line_dim, 1.0)
        next_middle = (
            middle
            + alpha_weight * from_before(upper, stride, line_dim, 0.0)
            + beta_weight * from_after(lower, stride, line_dim, 0.0)
        )
        next_lower = alpha_weight * from_before(lower, stride, line_dim, 0.0)
        next_upper = beta_weight * from_after(upper, stride, line_dim, 0.0)
        vectors = [
            vector
            + alpha_weight * from_before(vector, stride, line_dim, 0.0)
            + beta_weight * from_after(vector, stride, line_dim, 0.0)
            for vector in vectors
        ]
        lower, middle, upper = (next_lower, next_middle, next_upper)
        stride = stride * 2
    return [vector / middle for vector in vectors]


def edge_vector(coefficient, line_dim, leading):
    length = coefficient.shape[line_dim]
    position = lax.broadcasted_iota(jnp.int32, coefficient.shape, line_dim)
    target = 0 if leading else length - 1
    return jnp.where(position == target, coefficient, 0.0)


def matrix_product(left_matrix, right_matrix):
    return (
        left_matrix[0] * right_matrix[0] + left_matrix[1] * right_matrix[2],
        left_matrix[0] * right_matrix[1] + left_matrix[1] * right_matrix[3],
        left_matrix[2] * right_matrix[0] + left_matrix[3] * right_matrix[2],
        left_matrix[2] * right_matrix[1] + left_matrix[3] * right_matrix[3],
    )


def matrix_inverse(matrix):
    determinant = matrix[0] * matrix[3] - matrix[1] * matrix[2]
    return (
        matrix[3] / determinant,
        -matrix[1] / determinant,
        -matrix[2] / determinant,
        matrix[0] / determinant,
    )


def matrix_apply(matrix, vector):
    return (
        matrix[0] * vector[0] + matrix[1] * vector[1],
        matrix[2] * vector[0] + matrix[3] * vector[1],
    )


def shifted_identity(matrix, amount):
    return (matrix[0] + amount, matrix[1], matrix[2], matrix[3] + amount)


def negated(matrix):
    return tuple((-member for member in matrix))


def summed(first_part, second_part):
    return tuple(
        (
            first_member + second_member
            for first_member, second_member in zip(first_part, second_part)
        )
    )


def starting_rows(spike_list, end_list):
    lead_low, tail_low, lead_high, tail_high = spike_list
    nothing = jnp.zeros_like(lead_low)
    coefficients = (
        nothing,
        lead_low,
        nothing,
        tail_low,
        nothing,
        nothing,
        nothing,
        nothing,
        lead_high,
        nothing,
        tail_high,
        nothing,
    )
    return (coefficients, tuple(end_list))


def combine_rows(own_rows, below_rows, above_rows):
    own_coef, own_rhs = own_rows
    below_coef, below_rhs = below_rows
    above_coef, above_rhs = above_rows
    alpha_weight = negated(
        matrix_product(own_coef[0:4], matrix_inverse(shifted_identity(below_coef[4:8], 1.0)))
    )
    beta_weight = negated(
        matrix_product(own_coef[8:12], matrix_inverse(shifted_identity(above_coef[4:8], 1.0)))
    )
    next_lower = matrix_product(alpha_weight, below_coef[0:4])
    next_upper = matrix_product(beta_weight, above_coef[8:12])
    next_middle = summed(
        own_coef[4:8],
        summed(
            matrix_product(alpha_weight, below_coef[8:12]),
            matrix_product(beta_weight, above_coef[0:4]),
        ),
    )
    next_rhs = summed(
        own_rhs, summed(matrix_apply(alpha_weight, below_rhs), matrix_apply(beta_weight, above_rhs))
    )
    return (next_lower + next_middle + next_upper, next_rhs)


def final_values(system_rows):
    coefficients, rhs_values = system_rows
    return matrix_apply(matrix_inverse(shifted_identity(coefficients[4:8], 1.0)), rhs_values)


def solve_gathered(spike_stack, end_stack, position):
    devices = spike_stack.shape[0]
    system_rows = starting_rows(
        [spike_stack[:, entry] for entry in range(4)], [end_stack[:, 0], end_stack[:, 1]]
    )
    stride = 1
    while stride < devices:
        below_rows = jax.tree.map(lambda member: from_before(member, stride, 0, 0.0), system_rows)
        above_rows = jax.tree.map(lambda member: from_after(member, stride, 0, 0.0), system_rows)
        system_rows = combine_rows(system_rows, below_rows, above_rows)
        stride = stride * 2
    lead_all, tail_all = final_values(system_rows)
    tail_before = lax.dynamic_index_in_dim(
        from_before(tail_all, 1, 0, 0.0), position, 0, keepdims=False
    )
    lead_after = lax.dynamic_index_in_dim(
        from_after(lead_all, 1, 0, 0.0), position, 0, keepdims=False
    )
    return (tail_before, lead_after)


def shards(
    starting_thermal_values,
    horizontal_boundary_transmission,
    lateral_boundary_transmission,
    zaxis_interface_weight,
):
    layered_slices = starting_thermal_values.shape[2]
    bordered_thermal_mesh = with_halo(starting_thermal_values, (("gx", 0), ("gy", 1)), 1)
    first_edge = passed_along(horizontal_boundary_transmission[-1:], "gx", 1)
    second_edge = passed_along(lateral_boundary_transmission[:, -1:], "gy", 1)
    horizontal_below_band = jnp.concatenate([first_edge, horizontal_boundary_transmission[:-1]], 0)
    lateral_below_band = jnp.concatenate([second_edge, lateral_boundary_transmission[:, :-1]], 1)
    leading_flux = leading_speed * (
        horizontal_boundary_transmission[:, :, None]
        * (bordered_thermal_mesh[2:, 1:-1] - starting_thermal_values)
        - horizontal_below_band[:, :, None]
        * (starting_thermal_values - bordered_thermal_mesh[:-2, 1:-1])
    )
    trailing_flux = trailing_speed * (
        lateral_boundary_transmission[:, :, None]
        * (bordered_thermal_mesh[1:-1, 2:] - starting_thermal_values)
        - lateral_below_band[:, :, None]
        * (starting_thermal_values - bordered_thermal_mesh[1:-1, :-2])
    )
    increasing_ramp = starting_thermal_values[:, :, 1:] - starting_thermal_values[:, :, :-1]
    blank_vector_line = jnp.zeros(starting_thermal_values.shape[:2] + (1,), jnp.float32)
    third_flow = (
        third_rate
        * zaxis_interface_weight[:, :, None]
        * (
            jnp.concatenate([increasing_ramp, blank_vector_line], 2)
            - jnp.concatenate([blank_vector_line, increasing_ramp], 2)
        )
    )
    source = 2.0 * (leading_flux + trailing_flux + third_flow)
    whole_lines, line_faces = (
        lax.all_to_all(source, "gx", split_axis=1, concat_axis=0, tiled=True),
        lax.all_to_all(
            horizontal_boundary_transmission, "gx", split_axis=1, concat_axis=0, tiled=True
        ),
    )
    line_low = from_before(line_faces, 1, 0, 0.0)
    solved = reduce_lines(
        -leading_speed * line_low[:, :, None],
        1.0 + leading_speed * (line_low + line_faces)[:, :, None],
        -leading_speed * line_faces[:, :, None],
        [whole_lines],
        0,
    )[0]
    after_first = lax.all_to_all(solved, "gx", split_axis=0, concat_axis=1, tiled=True)
    second_lower = -trailing_speed * lateral_below_band[:, :, None]
    second_upper = -trailing_speed * lateral_boundary_transmission[:, :, None]
    second_middle = (
        1.0 + trailing_speed * (lateral_below_band + lateral_boundary_transmission)[:, :, None]
    )
    inside, spike_low, spike_high = reduce_lines(
        second_lower,
        second_middle,
        second_upper,
        [after_first, edge_vector(second_lower, 1, True), edge_vector(second_upper, 1, False)],
        1,
    )
    spike_list = [spike_low[:, 0], spike_low[:, -1], spike_high[:, 0], spike_high[:, -1]]
    end_list = [inside[:, 0], inside[:, -1]]
    gathered_spikes, gathered_ends = (
        lax.all_gather(jnp.stack(spike_list)[None], "gy", axis=0, tiled=True),
        lax.all_gather(jnp.stack(end_list)[None], "gy", axis=0, tiled=True),
    )
    tail_before, lead_after = solve_gathered(gathered_spikes, gathered_ends, lax.axis_index("gy"))
    after_second = inside - spike_low * tail_before[:, None] - spike_high * lead_after[:, None]
    depth = lax.broadcasted_iota(jnp.int32, (1, 1, layered_slices), 2)
    low_mask = (depth >= 1).astype(jnp.float32)
    high_mask = (depth < layered_slices - 1).astype(jnp.float32)
    vertical = third_rate * zaxis_interface_weight[:, :, None]
    final_pass_result = reduce_lines(
        -vertical * low_mask,
        1.0 + vertical * (low_mask + high_mask),
        -vertical * high_mask,
        [after_second],
        2,
    )[0]
    return starting_thermal_values + final_pass_result


def solution(mesh):
    in_specs = (P("gx", "gy", None), P("gx", "gy"), P("gx", "gy"), P("gx", "gy"))
    out_specs = P("gx", "gy", None)
    return jax.shard_map(shards, mesh=mesh, in_specs=in_specs, out_specs=out_specs, check_vma=False)
```

profile of v0, /device:TPU:0, one launch (start us, length us, event | category | flops | bytes accessed | tf_op | source)
XLA Modules:
  0.0 121.7 jit_solution(12748187560799751601)
XLA Ops:
  0.7 5.0 %collective-permute-start.1 = (f32[1,128]{1,0:T(1,128)S(1)}, f32[1,128]{1,0:T(1,128)S(1)}, u32[]{:S(2)}, u32[]{:S(2)}) collective-permute-start(f32[1,128]{1,0:T(1,128)S(1)} %slice.795), channel_id=1, source_target_pairs={{0,4},{4,8},{8,12},{12,16},{16,20},{20,24},{24,28},{1,5},{5,9},{9,... | collective-permute-start | bytes 1544 | tf_op jit(solution)/shard_map/ppermute | solution.py:27
  6.5 1.4 %collective-permute-start.4 = (f32[8,1]{1,0:T(8,128)S(1)}, f32[8,1]{1,0:T(8,128)S(1)}, u32[]{:S(2)}, u32[]{:S(2)}) collective-permute-start(f32[8,1]{1,0:T(8,128)S(1)} %slice.801), channel_id=1, source_target_pairs={{0,1},{1,2},{2,3},{4,5},{5,6},{6,7},{8,9},{9,10},{10,11},{12,13},{... | collective-permute-start | bytes 104 | tf_op jit(solution)/shard_map/ppermute | solution.py:27
  8.7 4.9 %all-to-all-start.1 = ((f32[8,1,128]{2,1,0:T(1,128)}), f32[8,1,128]{2,1,0:T(1,128)S(1)}, u32[]{:S(2)}, u32[]{:S(2)}) async-start(f32[8,1,128]{2,1,0:T(1,128)} %reshape.388), calls=%async_computation.1 | async-start | bytes 8192 | tf_op jit(solution)/shard_map/all_to_all | solution.py:230
  13.6 0.9 fusion.124
  14.4 1.3 %collective-permute-start = (f32[1,128,128]{2,1,0:T(8,128)S(1)}, f32[1,128,128]{2,1,0:T(8,128)S(1)}, u32[]{:S(2)}, u32[]{:S(2)}) collective-permute-start(f32[1,128,128]{2,1,0:T(8,128)S(1)} %get-tuple-element.190), channel_id=1, source_target_pairs={{4,0},{8,4},{12,8},{16,12},{20,16},{24,20},{28,24},{5,1},{9,5},{13... | collective-permute-start | bytes 196616 | tf_op jit(solution)/shard_map/ppermute | solution.py:19
  15.7 4.6 %collective-permute-start.2 = (f32[1,128,128]{2,1,0:T(8,128)S(1)}, f32[1,128,128]{2,1,0:T(8,128)S(1)}, u32[]{:S(2)}, u32[]{:S(2)}) collective-permute-start(f32[1,128,128]{2,1,0:T(8,128)S(1)} %get-tuple-element.191), channel_id=1, source_target_pairs={{0,4},{4,8},{8,12},{12,16},{16,20},{20,24},{24,28},{1,5},{5,9},{9,... | collective-permute-start | bytes 196616 | tf_op jit(solution)/shard_map/ppermute | solution.py:18
  21.0 1.4 %slice_subtract_fusion = f32[8,128,127]{2,1,0:T(8,128)S(1)} fusion(f32[8,128,128]{2,1,0:T(8,128)} %param.4), kind=kLoop, calls=%fused_computation.70 | loop fusion | flops 130048 | bytes 1560576 | tf_op jit(solution)/shard_map/sub | solution.py:217
  23.9 1.4 %fusion.104 = (f32[8,128,127]{2,1,0:T(8,128)S(1)}, f32[8,128,127]{2,1,0:T(8,128)}, f32[8,128,127]{2,1,0:T(8,128)}, f32[8,128,127]{2,1,0:T(8,128)}) fusion(f32[8,128,128]{2,1,0:T(8,128)S(1)} %get-tuple-element.275, f32[8,128,128]{2,1,0:T(8,128)S(1)} %get-tuple-element.274), kind=kLoop, calls=%fused_computation.359 | loop fusion | bytes 4161536 | tf_op jit(solution)/shard_map/slice | solution.py:35
  30.0 5.2 %all-gather = f32[16,8,1]{1,2,0:T(1,128)S(1)} all-gather(f32[4,8,1]{1,2,0:T(1,128)S(1)} %pad_maximum_fusion.7), channel_id=2, replica_groups=mesh['gx'=8,'gy'=4] {'gy'}, dimensions={0}, use_global_device_ids=true | all-gather | bytes 640 | tf_op jit(solution)/shard_map/all_gather | solution.py:258
  44.0 0.9 copy-done
  45.0 1.3 %collective-permute-start.3 = (f32[10,1,128]{2,1,0:T(1,128)S(1)}, f32[10,1,128]{2,1,0:T(1,128)S(1)}, u32[]{:S(2)}, u32[]{:S(2)}) collective-permute-start(f32[10,1,128]{2,1,0:T(1,128)S(1)} %get-tuple-element.108), channel_id=1, source_target_pairs={{1,0},{2,1},{3,2},{5,4},{6,5},{7,6},{9,8},{10,9},{11,10},{13,12},{... | collective-permute-start | bytes 15368 | tf_op jit(solution)/shard_map/ppermute | solution.py:19
  46.3 3.0 %collective-permute-start.5 = (f32[10,1,128]{2,1,0:T(1,128)S(1)}, f32[10,1,128]{2,1,0:T(1,128)S(1)}, u32[]{:S(2)}, u32[]{:S(2)}) collective-permute-start(f32[10,1,128]{2,1,0:T(1,128)S(1)} %get-tuple-element.109), channel_id=1, source_target_pairs={{0,1},{1,2},{2,3},{4,5},{5,6},{6,7},{8,9},{9,10},{10,11},{12,13},{... | collective-permute-start | bytes 15368 | tf_op jit(solution)/shard_map/ppermute | solution.py:18
  50.7 1.0 multiply_add_fusion.12
  51.8 1.1 copy.54
  52.9 6.0 %all-to-all-start = ((f32[8,128,128]{2,0,1:T(8,128)}), f32[8,128,128]{2,0,1:T(8,128)S(1)}, u32[]{:S(2)}, u32[]{:S(2)}) async-start(f32[8,128,128]{2,0,1:T(8,128)} %copy.54), calls=%async_computation | async-start | bytes 1048576 | tf_op jit(solution)/shard_map/all_to_all | solution.py:229
  59.0 15.6 %all-to-all-done = f32[8,128,128]{2,0,1:T(8,128)S(1)} async-done(((f32[8,128,128]{2,0,1:T(8,128)}), f32[8,128,128]{2,0,1:T(8,128)S(1)}, u32[]{:S(2)}, u32[]{:S(2)}) %all-to-all-start) | async-done | bytes 524320 | tf_op jit(solution)/shard_map/all_to_all | solution.py:229
  77.0 1.3 %add_divide_fusion.1 = f32[64,16,128]{2,1,0:T(8,128)} fusion(f32[32,16,128]{2,1,0:T(8,128)S(1)} %get-tuple-element.179, f32[64,16,128]{2,1,0:T(8,128)S(1)} %multiply_add_fusion.19, f32[32,16,128]{2,1,0:T(8,128)S(1)} %get-tuple-element.178, f32[64,16]{1,0:T(8,128)S(1)} %add_bitcast_fusion, f32[64,16]{1,0:T(8,128)S(1)} %get-tuple-element.85, ...), kind=kLoop, calls=%fused_computation.64 | loop fusion | flops 655360 | bytes 1585152 | tf_op jit(solution)/shard_map/div | solution.py:69
  78.4 3.8 %all-to-all-start.2 = ((f32[64,16,128]{2,1,0:T(8,128)}), f32[64,16,128]{2,1,0:T(8,128)S(1)}, u32[]{:S(2)}, u32[]{:S(2)}) async-start(f32[64,16,128]{2,1,0:T(8,128)} %add_divide_fusion.1), calls=%async_computation.2 | async-start | bytes 1048576 | tf_op jit(solution)/shard_map/all_to_all | solution.py:242
  84.0 13.1 %all-to-all-done.2 = f32[64,16,128]{2,1,0:T(8,128)S(1)} async-done(((f32[64,16,128]{2,1,0:T(8,128)}), f32[64,16,128]{2,1,0:T(8,128)S(1)}, u32[]{:S(2)}, u32[]{:S(2)}) %all-to-all-start.2) | async-done | bytes 524320 | tf_op jit(solution)/shard_map/all_to_all | solution.py:242
  100.2 5.4 %all-gather.1 = f32[8,8,128]{2,1,0:T(8,128)S(1)} all-gather(f32[2,8,128]{2,1,0:T(8,128)S(1)} %pad_maximum_fusion.4), channel_id=3, replica_groups=mesh['gx'=8,'gy'=4] {'gy'}, dimensions={0}, use_global_device_ids=true | all-gather | bytes 40960 | tf_op jit(solution)/shard_map/all_gather | solution.py:259
  107.2 0.8 copy-done.2
  108.2 1.2 multiply_add_fusion.10
  109.8 0.8 copy-done.1
  120.3 1.4 %divide_add_fusion = f32[8,128,128]{2,1,0:T(8,128)} fusion(f32[8,128,128]{2,1,0:T(8,128)S(1)} %copy-done, f32[8,128,64]{2,1,0:T(8,128)S(1)} %slice.1200, f32[8,128,128]{2,1,0:T(8,128)S(1)} %get-tuple-element.106, f32[8,128,64]{2,1,0:T(8,128)S(1)} %bitcast.219, f32[8,128,64]{2,1,0:T(8,128)S(1)} %get-tuple-element.113, ...), kind=kLoop, calls=%fused_computation.18 | loop fusion | flops 1835008 | bytes 4718592 | tf_op jit(solution)/shard_map/add | solution.py:274
  (362 shorter events, 37.2 us)
Async XLA Ops:
  0.7 7.2 %copy-start.5 = (f32[8,128]{1,0:T(8,128)S(1)}, f32[8,128]{1,0:T(8,128)}, u32[]{:S(2)}) copy-start(f32[8,128]{1,0:T(8,128)} %param.5) | copy-start | bytes 12292
  0.7 41.4 %collective-permute-start.1 = (f32[1,128]{1,0:T(1,128)S(1)}, f32[1,128]{1,0:T(1,128)S(1)}, u32[]{:S(2)}, u32[]{:S(2)}) collective-permute-start(f32[1,128]{1,0:T(1,128)S(1)} %slice.795), channel_id=1, source_target_pairs={{0,4},{4,8},{8,12},{12,16},{16,20},{20,24},{24,28},{1,5},{5,9},{9,... | collective-permute-start | bytes 1544 | tf_op jit(solution)/shard_map/ppermute | solution.py:27
  6.5 18.9 %collective-permute-start.4 = (f32[8,1]{1,0:T(8,128)S(1)}, f32[8,1]{1,0:T(8,128)S(1)}, u32[]{:S(2)}, u32[]{:S(2)}) collective-permute-start(f32[8,1]{1,0:T(8,128)S(1)} %slice.801), channel_id=1, source_target_pairs={{0,1},{1,2},{2,3},{4,5},{5,6},{6,7},{8,9},{9,10},{10,11},{12,13},{... | collective-permute-start | bytes 104 | tf_op jit(solution)/shard_map/ppermute | solution.py:27
  8.7 33.4 %all-to-all-start.1 = ((f32[8,1,128]{2,1,0:T(1,128)}), f32[8,1,128]{2,1,0:T(1,128)S(1)}, u32[]{:S(2)}, u32[]{:S(2)}) async-start(f32[8,1,128]{2,1,0:T(1,128)} %reshape.388), calls=%async_computation.1 | async-start | bytes 8192 | tf_op jit(solution)/shard_map/all_to_all | solution.py:230
  14.4 30.5 %collective-permute-start = (f32[1,128,128]{2,1,0:T(8,128)S(1)}, f32[1,128,128]{2,1,0:T(8,128)S(1)}, u32[]{:S(2)}, u32[]{:S(2)}) collective-permute-start(f32[1,128,128]{2,1,0:T(8,128)S(1)} %get-tuple-element.190), channel_id=1, source_target_pairs={{4,0},{8,4},{12,8},{16,12},{20,16},{24,20},{28,24},{5,1},{9,5},{13... | collective-permute-start | bytes 196616 | tf_op jit(solution)/shard_map/ppermute | solution.py:19
  15.7 28.2 %collective-permute-start.2 = (f32[1,128,128]{2,1,0:T(8,128)S(1)}, f32[1,128,128]{2,1,0:T(8,128)S(1)}, u32[]{:S(2)}, u32[]{:S(2)}) collective-permute-start(f32[1,128,128]{2,1,0:T(8,128)S(1)} %get-tuple-element.191), channel_id=1, source_target_pairs={{0,4},{4,8},{8,12},{12,16},{16,20},{20,24},{24,28},{1,5},{5,9},{9,... | collective-permute-start | bytes 196616 | tf_op jit(solution)/shard_map/ppermute | solution.py:18
  36.8 4.1 %copy-start.46 = (f32[4,8,1]{1,0,2:T(4,128)}, f32[4,8,1]{1,0,2:T(4,128)S(1)}, u32[]{:S(2)}) copy-start(f32[4,8,1]{1,0,2:T(4,128)S(1)} %get-tuple-element.257) | copy-start | bytes 388
  36.8 4.7 %copy-start.48 = (f32[4,8,1]{1,0,2:T(4,128)}, f32[4,8,1]{1,0,2:T(4,128)S(1)}, u32[]{:S(2)}) copy-start(f32[4,8,1]{1,0,2:T(4,128)S(1)} %get-tuple-element.273) | copy-start | bytes 388
  45.0 4.4 %collective-permute-start.3 = (f32[10,1,128]{2,1,0:T(1,128)S(1)}, f32[10,1,128]{2,1,0:T(1,128)S(1)}, u32[]{:S(2)}, u32[]{:S(2)}) collective-permute-start(f32[10,1,128]{2,1,0:T(1,128)S(1)} %get-tuple-element.108), channel_id=1, source_target_pairs={{1,0},{2,1},{3,2},{5,4},{6,5},{7,6},{9,8},{10,9},{11,10},{13,12},{... | collective-permute-start | bytes 15368 | tf_op jit(solution)/shard_map/ppermute | solution.py:19
  46.3 3.8 %collective-permute-start.5 = (f32[10,1,128]{2,1,0:T(1,128)S(1)}, f32[10,1,128]{2,1,0:T(1,128)S(1)}, u32[]{:S(2)}, u32[]{:S(2)}) collective-permute-start(f32[10,1,128]{2,1,0:T(1,128)S(1)} %get-tuple-element.109), channel_id=1, source_target_pairs={{0,1},{1,2},{2,3},{4,5},{5,6},{6,7},{8,9},{9,10},{10,11},{12,13},{... | collective-permute-start | bytes 15368 | tf_op jit(solution)/shard_map/ppermute | solution.py:18
  52.9 21.8 %all-to-all-start = ((f32[8,128,128]{2,0,1:T(8,128)}), f32[8,128,128]{2,0,1:T(8,128)S(1)}, u32[]{:S(2)}, u32[]{:S(2)}) async-start(f32[8,128,128]{2,0,1:T(8,128)} %copy.54), calls=%async_computation | async-start | bytes 1048576 | tf_op jit(solution)/shard_map/all_to_all | solution.py:229
  78.2 4.1 %copy-start.41 = (f32[4,8,1]{1,0,2:T(4,128)S(1)}, f32[4,8,1]{1,0,2:T(4,128)}, u32[]{:S(2)}) copy-start(f32[4,8,1]{1,0,2:T(4,128)} %copy-done.40) | copy-start | bytes 388
  78.4 4.6 %copy-start.36 = (f32[4,8,1]{1,0,2:T(4,128)S(1)}, f32[4,8,1]{1,0,2:T(4,128)}, u32[]{:S(2)}) copy-start(f32[4,8,1]{1,0,2:T(4,128)} %copy-done.35) | copy-start | bytes 388
  78.4 4.6 %copy-start.45 = (f32[4,8,1]{1,0,2:T(4,128)S(1)}, f32[4,8,1]{1,0,2:T(4,128)}, u32[]{:S(2)}) copy-start(f32[4,8,1]{1,0,2:T(4,128)} %copy-done.44) | copy-start | bytes 388
  78.4 4.6 %copy-start.47 = (f32[4,8,1]{1,0,2:T(4,128)S(1)}, f32[4,8,1]{1,0,2:T(4,128)}, u32[]{:S(2)}) copy-start(f32[4,8,1]{1,0,2:T(4,128)} %copy-done.46) | copy-start | bytes 388
  78.4 4.6 %copy-start.49 = (f32[4,8,1]{1,0,2:T(4,128)S(1)}, f32[4,8,1]{1,0,2:T(4,128)}, u32[]{:S(2)}) copy-start(f32[4,8,1]{1,0,2:T(4,128)} %copy-done.48) | copy-start | bytes 388
  78.4 4.6 %copy-start.51 = (f32[4,8,1]{1,0,2:T(4,128)S(1)}, f32[4,8,1]{1,0,2:T(4,128)}, u32[]{:S(2)}) copy-start(f32[4,8,1]{1,0,2:T(4,128)} %copy-done.50) | copy-start | bytes 388
  78.4 4.6 %copy-start.70 = (f32[2,8,1]{1,0,2:T(2,128)S(1)}, f32[2,8,1]{1,0,2:T(2,128)}, u32[]{:S(2)}) copy-start(f32[2,8,1]{1,0,2:T(2,128)} %slice.976) | copy-start | bytes 196
  78.4 4.6 %copy-start.71 = (f32[2,8,1]{1,0,2:T(2,128)S(1)}, f32[2,8,1]{1,0,2:T(2,128)}, u32[]{:S(2)}) copy-start(f32[2,8,1]{1,0,2:T(2,128)} %slice.978) | copy-start | bytes 196
  78.4 18.6 %all-to-all-start.2 = ((f32[64,16,128]{2,1,0:T(8,128)}), f32[64,16,128]{2,1,0:T(8,128)S(1)}, u32[]{:S(2)}, u32[]{:S(2)}) async-start(f32[64,16,128]{2,1,0:T(8,128)} %add_divide_fusion.1), calls=%async_computation.2 | async-start | bytes 1048576 | tf_op jit(solution)/shard_map/all_to_all | solution.py:242
  99.7 5.9 %copy-start.18 = (f32[4,1,8,1]{2,1,0,3:T(1,128)S(1)}, f32[4,1,8,1]{2,1,0,3:T(1,128)}, u32[]{:S(2)}) copy-start(f32[4,1,8,1]{2,1,0,3:T(1,128)} %copy-done.17) | copy-start | bytes 388
  99.7 5.9 %copy-start.20 = (f32[4,1,8,1]{2,1,0,3:T(1,128)S(1)}, f32[4,1,8,1]{2,1,0,3:T(1,128)}, u32[]{:S(2)}) copy-start(f32[4,1,8,1]{2,1,0,3:T(1,128)} %copy-done.19) | copy-start | bytes 388
  99.7 5.9 %copy-start.22 = (f32[4,1,8,1]{2,1,0,3:T(1,128)S(1)}, f32[4,1,8,1]{2,1,0,3:T(1,128)}, u32[]{:S(2)}) copy-start(f32[4,1,8,1]{2,1,0,3:T(1,128)} %copy-done.21) | copy-start | bytes 388
  99.7 5.9 %copy-start.24 = (f32[4,1,8,1]{2,1,0,3:T(1,128)S(1)}, f32[4,1,8,1]{2,1,0,3:T(1,128)}, u32[]{:S(2)}) copy-start(f32[4,1,8,1]{2,1,0,3:T(1,128)} %copy-done.23) | copy-start | bytes 388
  (59 other events, 118.3 us)
where the time goes:
time: 123 us; the launch traced here: 122 us
  starting transfers between devices  31.3 us (25%)
  waiting for transfers between devices  29.4 us (24%)
  local copies, waits for them, and re-layouts  27.8 us (23%)
  other arithmetic  20.8 us (17%)
  blocking collectives  10.6 us (9%)
  between operations  1.74 us (1%)
    all_to_all x1, waiting for transfers between devices, shards(): lax.all_to_all(source, 'gx', split_axis=1, concat_axis=0, tiled=True)  15.6 us
    all_to_all x1, waiting for transfers between devices, shards(): lax.all_to_all(solved, 'gx', split_axis=0, concat_axis=1, tiled=True)  13.1 us
    slice x63, local copies, waits for them, and re-layouts, from_before(): retained = lax.slice_in_dim(values, 0, length - stride, axis=line_dim)  8.46 us
    slice x51, local copies, waits for them, and re-layouts, from_after(): retained = lax.slice_in_dim(values, stride, length, axis=line_dim)  7.82 us
    ppermute x2, starting transfers between devices, with_halo(): before = lax.ppermute(last, axis, up)  7.59 us
    add x23, other arithmetic, reduce_lines(): vector + alpha_weight * from_before(vector, stride, line_dim, 0.0)  7.58 us
    unnamed x152, local copies, waits for them, and re-layouts  6.86 us
    ppermute x2, starting transfers between devices, passed_along(): return lax.ppermute(block, axis, route)  6.44 us
  transfers between devices with their start and end apart: 9, of which 3 were waited for; matrix products, arithmetic and copies ran while one was open for 16% of the time, Pallas kernels for 0%

commit v1 on v0

v1 whole, which is shorter than its diff:
```python
import functools

import jax
import jax.numpy as jnp
import numpy as np
from jax import lax
from jax.experimental import pallas as pl
from jax.experimental.pallas import tpu as pltpu
from jax.sharding import PartitionSpec as P

R1 = 40000.0
R2 = 40000.0
R3 = 0.25
MESH = pl.DeviceIdType.MESH


def dot(a, b):
    return jnp.dot(a, b, precision=lax.Precision.HIGHEST, preferred_element_type=jnp.float32)


def kernel(
    dx, dy,
    u, p, q, w, basis, basis_t, mu, out,
    uh, xl, pall, gbuf, grecv, summ, rin, rout, zx, ysum, yall, ca, cat, cb, cbt, rho_s, ipi_s,
    scan_s, edge_s,
    p_send, p_recv, g_send, g_recv, a_send, a_recv, b_send, b_recv, y_send, y_recv,
):
    nx, ny, nz = u.shape
    chunk = ny // dx
    mx, my = lax.axis_index("gx"), lax.axis_index("gy")

    gbuf[0] = u[:, 0, :]
    gbuf[1] = u[:, ny - 1, :]
    gbuf[2] = q[...]

    barrier = pltpu.get_barrier_semaphore()
    for off in range(1, dx):
        pl.semaphore_signal(
            barrier, inc=1, device_id={"gx": lax.rem(mx + off, dx)}, device_id_type=MESH
        )
    for off in range(1, dy):
        pl.semaphore_signal(
            barrier, inc=1, device_id={"gy": lax.rem(my + off, dy)}, device_id_type=MESH
        )
    pl.semaphore_wait(barrier, dx + dy - 2)

    def send(src, dst, ssem, rsem, axis, peer):
        copy = pltpu.make_async_remote_copy(
            src_ref=src, dst_ref=dst, send_sem=ssem, recv_sem=rsem,
            device_id={axis: peer}, device_id_type=MESH,
        )
        copy.start()
        return copy

    p_copies = [
        send(p, pall.at[mx], p_send.at[o], p_recv.at[o], "gx", lax.rem(mx + o, dx))
        for o in range(1, dx)
    ]
    g_copies = [
        send(gbuf, grecv.at[my], g_send.at[o], g_recv.at[o], "gy", lax.rem(my + o, dy))
        for o in range(1, dy)
    ]
    pall[mx] = p[...]
    grecv[my] = gbuf[...]

    uh[...] = dot(u[...].reshape(nx * ny, nz), basis[...]).reshape(nx, ny, nz)

    for copy in g_copies:
        copy.wait()

    g = R2 * grecv[:, 2].reshape(dy * nx, ny)
    lane = lax.broadcasted_iota(jnp.int32, (dy * nx, ny), 1)
    scale = 1.0 / (2.0 + 3.0 * g)
    a, b, c, d = (1.0 + g) * scale, g * scale, scale, g * scale
    stride = 1
    while stride < ny:
        ar, br, cr, dr = (pltpu.roll(m, stride, 1) for m in (a, b, c, d))
        na, nb, nc, nd = a * ar + b * cr, a * br + b * dr, c * ar + d * cr, c * br + d * dr
        scale = 1.0 / (na + nb + nc + nd)
        keep = lane >= stride
        a, b, c, d = (
            jnp.where(keep, n * scale, o)
            for n, o in ((na, a), (nb, b), (nc, c), (nd, d))
        )
        stride *= 2
    sigma_in = jnp.ones((nx, 1), jnp.float32)
    for k in range(dy - 1):
        rows = slice(k * nx, (k + 1) * nx)
        ta, tb, tc, td = (m[rows, ny - 1 :] for m in (a, b, c, d))
        sigma_in = jnp.where(
            k < my, (ta * sigma_in + tb) / (tc * sigma_in + td), sigma_in
        )
    for k, m in enumerate((a, b, c, d)):
        scan_s[k] = pltpu.roll(m, 1, 1).reshape(dy, nx, ny)
    lane = lax.broadcasted_iota(jnp.int32, (nx, ny), 1)
    a, b, c, d = (scan_s[k, my] for k in range(4))
    sigma = jnp.where(lane == 0, sigma_in, (a * sigma_in + b) / (c * sigma_in + d))
    g = R2 * q[...]
    ipi = 1.0 / (g + sigma)
    prefix = g * ipi
    stride = 1
    while stride < ny:
        prefix = jnp.where(lane >= stride, prefix * pltpu.roll(prefix, stride, 1), prefix)
        stride *= 2
    total = prefix[:, ny - 1 :]
    before = jnp.where(lane == 0, 1.0, pltpu.roll(prefix, 1, 1))
    inverse = 1.0 / before
    row_i = lax.broadcasted_iota(jnp.int32, (ny, ny), 0)
    col_i = lax.broadcasted_iota(jnp.int32, (ny, ny), 1)
    lower = jnp.where(row_i >= col_i, 1.0, 0.0)
    upper = jnp.where(row_i <= col_i, 1.0, 0.0)
    weight = before * before * ipi
    a2 = inverse * dot(weight, lower)
    b2 = inverse * total
    cb[...] = jnp.zeros_like(cb)
    for k, m in enumerate((g, R3 * w[...], inverse, weight, a2, b2)):
        cb[k * nx : (k + 1) * nx] = m
    cbt[...] = cb[...].T

    ysum[2] = jnp.broadcast_to(total, (nx, nz))
    ysum[3] = jnp.broadcast_to(a2[:, 0:1], (nx, nz))

    prev, following = lax.rem(my + dy - 1, dy), lax.rem(my + 1, dy)
    low_u = dot(grecv[prev, 1], basis[...])
    high_u = jnp.where(my == dy - 1, 0.0, dot(grecv[following, 0], basis[...]))
    q_before = jnp.where(my == 0, 0.0, R2 * grecv[prev, 2][:, ny - 1 :])
    first_u = dot(gbuf[0], basis[...])
    edge_s[0] = q_before * (first_u - low_u)
    edge_s[1] = high_u

    for copy in p_copies:
        copy.wait()
    sigma = jnp.ones((1, ny), jnp.float32)
    for k in range(dx):
        block = R1 * pall[k]
        rhos, ipis = [], []
        for r in range(nx):
            gr = block[r : r + 1]
            inv = 1.0 / (gr + sigma)
            rho = gr * inv
            sigma = 1.0 + rho * sigma
            rhos.append(rho)
            ipis.append(inv)
        rho_s[k] = jnp.concatenate(rhos, 0)
        ipi_s[k] = jnp.concatenate(ipis, 0)

    def responses(rho, ipi):
        prod = [jnp.ones_like(rho[0])]
        for r in range(nx):
            prod.append(prod[r] * rho[r])
        resp, tail = [None] * nx, [None] * nx
        resp[nx - 1], tail[nx - 1] = prod[nx - 1] * ipi[nx - 1], rho[nx - 1]
        for r in range(nx - 2, -1, -1):
            resp[r] = prod[r] * ipi[r] + rho[r] * resp[r + 1]
            tail[r] = rho[r] * tail[r + 1]
        return resp, tail

    resp, tail = responses(
        [rho_s[:, r, :] for r in range(nx)], [ipi_s[:, r, :] for r in range(nx)]
    )
    ca[...] = jnp.zeros_like(ca)
    base = 4 * nx
    ca[base : base + dx] = tail[0]
    ca[base + dx : base + 2 * dx] = resp[0]
    rho, ipi = rho_s[mx], ipi_s[mx]
    resp, tail = responses(
        [rho[r : r + 1] for r in range(nx)], [ipi[r : r + 1] for r in range(nx)]
    )
    ca[0:nx] = rho
    ca[nx : 2 * nx] = ipi
    ca[2 * nx : 3 * nx] = jnp.concatenate(resp, 0)
    ca[3 * nx : 4 * nx] = jnp.concatenate(tail, 0)
    cat[...] = ca[...].T

    row = lax.broadcasted_iota(jnp.int32, (ny, nz), 0)
    z = None
    for r in range(nx):
        v = uh[r]
        gc = cbt[:, r : r + 1]
        wc = cbt[:, nx + r : nx + r + 1]
        after = jnp.where(row == ny - 1, edge_s[1, r : r + 1, :], pltpu.roll(v, ny - 1, 0))
        flux = gc * (after - v)
        flux_before = jnp.where(row == 0, edge_s[0, r : r + 1, :], pltpu.roll(flux, 1, 0))
        h = (flux - flux_before) + (v - (wc * mu[...]) * v)
        z = h if r == 0 else h + cat[:, r - 1 : r] * z
        xl[r] = z
    summ[0] = cat[:, nx - 1 : nx] * z
    x = z * cat[:, 2 * nx - 1 : 2 * nx]
    xl[nx - 1] = x
    for r in range(nx - 2, -1, -1):
        x = xl[r] * cat[:, nx + r : nx + r + 1] + cat[:, r : r + 1] * x
        xl[r] = x
    summ[1] = x

    def part(index):
        return pl.ds(pl.multiple_of(index * chunk, chunk), chunk)

    copies = []
    for o in range(1, dx):
        peer = lax.rem(mx + o, dx)
        copies.append(
            send(summ.at[:, part(peer), :], rin.at[mx], a_send.at[o], a_recv.at[o], "gx", peer)
        )
    rin[mx] = summ[:, part(mx), :]
    for copy in copies:
        copy.wait()
    own = cat[part(mx), :]
    carry = jnp.zeros((chunk, nz), jnp.float32)
    carries = []
    for k in range(dx):
        carries.append(carry)
        rout[k, 0] = carry
        carry = rin[k, 0] + own[:, base + k : base + k + 1] * carry
    carry = jnp.zeros((chunk, nz), jnp.float32)
    for k in range(dx - 1, -1, -1):
        rout[k, 1] = carry
        carry = (
            rin[k, 1]
            + own[:, base + dx + k : base + dx + k + 1] * carries[k]
            + own[:, base + k : base + k + 1] * carry
        )
    copies = []
    for o in range(1, dx):
        peer = lax.rem(mx + o, dx)
        copies.append(
            send(rout.at[peer], zx.at[:, part(mx), :], b_send.at[o], b_recv.at[o], "gx", peer)
        )
    zx[:, part(mx), :] = rout[mx]
    for copy in copies:
        copy.wait()

    for r in range(nx):
        x = (
            xl[r]
            + cat[:, 2 * nx + r : 2 * nx + r + 1] * zx[0]
            + cat[:, 3 * nx + r : 3 * nx + r + 1] * zx[1]
        )
        f = 2.0 * (x - uh[r])
        inv = cbt[:, 2 * nx + r : 2 * nx + r + 1]
        s = dot(lower, inv * f)
        ysum[0, r : r + 1, :] = s[ny - 1 :]
        y = inv * dot(upper, cbt[:, 3 * nx + r : 3 * nx + r + 1] * s)
        ysum[1, r : r + 1, :] = y[0:1]
        xl[r] = y
    copies = [
        send(ysum, yall.at[my], y_send.at[o], y_recv.at[o], "gy", lax.rem(my + o, dy))
        for o in range(1, dy)
    ]
    yall[my] = ysum[...]
    for copy in copies:
        copy.wait()
    carry = jnp.zeros((nx, nz), jnp.float32)
    zeta, carries = carry, []
    for k in range(dy):
        carries.append(carry)
        zeta = jnp.where(k == my, carry, zeta)
        carry = yall[k, 2] * (yall[k, 0] + carry)
    carry = jnp.zeros((nx, nz), jnp.float32)
    xi = carry
    for k in range(dy - 1, -1, -1):
        xi = jnp.where(k == my, carry, xi)
        carry = yall[k, 1] + yall[k, 3] * carries[k] + yall[k, 2] * carry

    for r in range(nx):
        v = (
            xl[r]
            + cbt[:, 4 * nx + r : 4 * nx + r + 1] * zeta[r : r + 1]
            + cbt[:, 5 * nx + r : 5 * nx + r + 1] * xi[r : r + 1]
        )
        v = v / (1.0 + cbt[:, nx + r : nx + r + 1] * mu[...])
        out[r] = u[r] + dot(v, basis_t[...])


def shards(dx, dy, u, p, q, w):
    nx, ny, nz = u.shape
    mode = np.arange(nz)
    basis = np.cos(np.pi * mode[None, :] * (mode[:, None] + 0.5) / nz) * np.sqrt(2.0 / nz)
    basis[:, 0] *= np.sqrt(0.5)
    mu = (2.0 - 2.0 * np.cos(np.pi * mode / nz))[None, :]
    basis_t = jnp.asarray(basis.T, jnp.float32)
    basis = jnp.asarray(basis, jnp.float32)
    mu = jnp.asarray(mu, jnp.float32)
    chunk = ny // dx
    f32 = lambda *shape: pltpu.VMEM(shape, jnp.float32)
    rows = -(-(4 * nx + 2 * dx) // 128) * 128
    sems = []
    for count in (dx, dy, dx, dx, dy):
        sems += [pltpu.SemaphoreType.DMA((count,))] * 2
    vmem = pl.BlockSpec(memory_space=pltpu.VMEM)
    return pl.pallas_call(
        functools.partial(kernel, dx, dy),
        out_shape=jax.ShapeDtypeStruct(u.shape, jnp.float32),
        in_specs=[vmem] * 7,
        out_specs=vmem,
        scratch_shapes=[
            f32(nx, ny, nz), f32(nx, ny, nz), f32(dx, nx, ny), f32(3, nx, ny),
            f32(dy, 3, nx, ny), f32(2, ny, nz), f32(dx, 2, chunk, nz), f32(dx, 2, chunk, nz),
            f32(2, ny, nz), f32(4, nx, nz), f32(dy, 4, nx, nz),
            f32(rows, ny), f32(ny, rows), f32(rows, ny), f32(ny, rows),
            f32(dx, nx, ny), f32(dx, nx, ny), f32(4, dy, nx, ny), f32(2, nx, nz),
        ] + sems,
        compiler_params=pltpu.CompilerParams(
            collective_id=0, has_side_effects=True, vmem_limit_bytes=48 * 2**20
        ),
    )(u, p, q, w, basis, basis_t, mu)


def solution(mesh):
    dx, dy = mesh.shape["gx"], mesh.shape["gy"]
    in_specs = (P("gx", "gy", None), P("gx", "gy"), P("gx", "gy"), P("gx", "gy"))
    return jax.shard_map(
        functools.partial(shards, dx, dy), mesh=mesh, in_specs=in_specs,
        out_specs=P("gx", "gy", None), check_vma=False,
    )
```

time: 123 us -> 34.2 us (0.28)
  starting transfers between devices: 31.3 us -> 0 us
  waiting for transfers between devices: 29.4 us -> 0 us
  Pallas kernels: 0 us -> 27.6 us
  local copies, waits for them, and re-layouts: 27.8 us -> 6.23 us
  other arithmetic: 20.8 us -> 0 us
  blocking collectives: 10.6 us -> 0 us
  between operations: 1.74 us -> 0.02 us
    all_to_all x3 -> x0, waiting for transfers between devices: 28.7 us -> none  [the longest x1 15.6 us: shards(): lax.all_to_all(source, 'gx', split_axis=1, concat_axis=0, tiled=True)]
    pallas_call x0 -> x1, Pallas kernels: none -> 27.6 us  [shards(): pl.pallas_call(functools.partial(kernel, dx, dy), out_shape=jax.ShapeDtyp...]
    slice x121 -> x0, local copies, waits for them, and re-layouts: 19 us -> none  [the longest x63 8.46 us: from_before(): retained = lax.slice_in_dim(values, 0, length - stride, axis=line_dim)]
    ppermute x6 -> x0, starting transfers between devices: 16.6 us -> none  [the longest x2 7.59 us: with_halo(): before = lax.ppermute(last, axis, up)]
    all_to_all x3 -> x0, starting transfers between devices: 14.7 us -> none  [the longest x1 6.01 us: shards(): lax.all_to_all(source, 'gx', split_axis=1, concat_axis=0, tiled=True)]
    add x47 -> x0, other arithmetic: 14.1 us -> none  [the longest x23 7.58 us: reduce_lines(): vector + alpha_weight * from_before(vector, stride, line_dim, 0.0)]
    all_gather x2 -> x0, blocking collectives: 10.6 us -> none  [the longest x1 5.37 us: shards(): lax.all_gather(jnp.stack(end_list)[None], 'gy', axis=0, tiled=True)]
    div x5 -> x0, other arithmetic: 1.94 us -> none  [reduce_lines(): return [vector / middle for vector in vectors]]
  transfers between devices with their start and end apart: 9 -> 0, of which waited for: 3 -> 0; matrix products, arithmetic and copies ran while one was open for 16% -> 0% of each run, Pallas kernels for 0% -> 0%
where the time goes in v1:
time: 34.2 us; the launch traced here: 33.9 us
  Pallas kernels  27.6 us (81%)
  local copies, waits for them, and re-layouts  6.23 us (18%)
    pallas_call x1, Pallas kernels, shards(): pl.pallas_call(functools.partial(kernel, dx, dy), out_shape=jax.ShapeDtyp...  27.6 us
    unnamed x15, local copies, waits for them, and re-layouts  6.23 us

profile of v1, /device:TPU:0, one launch (start us, length us, event | category | flops | bytes accessed | tf_op | source)
XLA Modules:
  0.0 33.9 jit_solution(65500674739560341)
XLA Ops:
  0.0 0.0 copy-start.6
  0.0 0.7 %copy-done.6 = f32[1,128]{1,0:T(1,128)S(1)} copy-done((f32[1,128]{1,0:T(1,128)S(1)}, f32[1,128]{1,0:T(1,128)}, u32[]{:S(2)}) %copy-start.6) | copy-done | bytes 536
  0.7 0.0 copy-start
  0.7 1.0 %copy-done = f32[8,128,128]{2,1,0:T(8,128)S(1)} copy-done((f32[8,128,128]{2,1,0:T(8,128)S(1)}, f32[8,128,128]{2,1,0:T(8,128)}, u32[]{:S(2)}) %copy-start) | copy-done | bytes 524312
  1.7 0.0 copy-start.1
  1.7 0.8 %copy-done.1 = f32[128,128]{1,0:T(8,128)S(1)} copy-done((f32[128,128]{1,0:T(8,128)S(1)}, f32[128,128]{1,0:T(8,128)}, u32[]{:S(2)}) %copy-start.1) | copy-done | bytes 65560
  2.5 0.0 copy-start.2
  2.5 0.8 %copy-done.2 = f32[128,128]{1,0:T(8,128)S(1)} copy-done((f32[128,128]{1,0:T(8,128)S(1)}, f32[128,128]{1,0:T(8,128)}, u32[]{:S(2)}) %copy-start.2) | copy-done | bytes 65560
  3.4 0.0 copy-start.3
  3.4 0.7 %copy-done.3 = f32[8,128]{1,0:T(8,128)S(1)} copy-done((f32[8,128]{1,0:T(8,128)S(1)}, f32[8,128]{1,0:T(8,128)}, u32[]{:S(2)}) %copy-start.3) | copy-done | bytes 4120
  4.1 0.0 copy-start.4
  4.1 0.7 %copy-done.4 = f32[8,128]{1,0:T(8,128)S(1)} copy-done((f32[8,128]{1,0:T(8,128)S(1)}, f32[8,128]{1,0:T(8,128)}, u32[]{:S(2)}) %copy-start.4) | copy-done | bytes 4120
  4.8 0.0 copy-start.5
  4.8 0.7 %copy-done.5 = f32[8,128]{1,0:T(8,128)S(1)} copy-done((f32[8,128]{1,0:T(8,128)S(1)}, f32[8,128]{1,0:T(8,128)}, u32[]{:S(2)}) %copy-start.5) | copy-done | bytes 4120
  5.4 27.6 %shard_map.73 = f32[8,128,128]{2,1,0:T(8,128)S(1)} custom-call(f32[8,128,128]{2,1,0:T(8,128)S(1)} %copy-done, f32[8,128]{1,0:T(8,128)S(1)} %copy-done.3, f32[8,128]{1,0:T(8,128)S(1)} %copy-done.4, f32[8,128]{1,0:T(8,128)S(1)} %copy-done.5, f32[128,128]{1,0:T(8,128)S(1)} %copy-done.1, f32[128,128]{1,0:T(8,128)S(1)} %copy-done.2, f32[1,128]{1,0:T(1,128)S(1)} %copy-done.6), custom_call_target="tpu_custom_call" | custom-call | tf_op jit(solution)/shard_map/pallas_call | solution.py:290
  33.1 0.8 %copy.9 = f32[8,128,128]{2,1,0:T(8,128)} copy(f32[8,128,128]{2,1,0:T(8,128)S(1)} %shard_map.73) | data formatting | bytes 1048576
Async XLA Ops:
  0.0 0.7 %copy-start.6 = (f32[1,128]{1,0:T(1,128)S(1)}, f32[1,128]{1,0:T(1,128)}, u32[]{:S(2)}) copy-start(f32[1,128]{1,0:T(1,128)} %constant.8.clone.mu) | copy-start | bytes 1540
  0.7 1.0 %copy-start = (f32[8,128,128]{2,1,0:T(8,128)S(1)}, f32[8,128,128]{2,1,0:T(8,128)}, u32[]{:S(2)}) copy-start(f32[8,128,128]{2,1,0:T(8,128)} %u.1) | copy-start | bytes 1572868
  1.7 0.8 %copy-start.1 = (f32[128,128]{1,0:T(8,128)S(1)}, f32[128,128]{1,0:T(8,128)}, u32[]{:S(2)}) copy-start(f32[128,128]{1,0:T(8,128)} %constant.7.clone.basis) | copy-start | bytes 196612
  2.5 0.8 %copy-start.2 = (f32[128,128]{1,0:T(8,128)S(1)}, f32[128,128]{1,0:T(8,128)}, u32[]{:S(2)}) copy-start(f32[128,128]{1,0:T(8,128)} %constant.6.clone.basis_t) | copy-start | bytes 196612
  3.4 0.7 %copy-start.3 = (f32[8,128]{1,0:T(8,128)S(1)}, f32[8,128]{1,0:T(8,128)}, u32[]{:S(2)}) copy-start(f32[8,128]{1,0:T(8,128)} %p.1) | copy-start | bytes 12292
  4.1 0.7 %copy-start.4 = (f32[8,128]{1,0:T(8,128)S(1)}, f32[8,128]{1,0:T(8,128)}, u32[]{:S(2)}) copy-start(f32[8,128]{1,0:T(8,128)} %q.1) | copy-start | bytes 12292
  4.8 0.7 %copy-start.5 = (f32[8,128]{1,0:T(8,128)S(1)}, f32[8,128]{1,0:T(8,128)}, u32[]{:S(2)}) copy-start(f32[8,128]{1,0:T(8,128)} %w.1) | copy-start | bytes 12292

commit v2 on v1

v2 whole, which is shorter than its diff:
```python
import functools

import jax
import jax.numpy as jnp
import numpy as np
from jax import lax
from jax.experimental import pallas as pl
from jax.experimental.pallas import tpu as pltpu
from jax.sharding import PartitionSpec as P

R1 = 40000.0
R2 = 40000.0
R3 = 0.25
MESH = pl.DeviceIdType.MESH


def dot(a, b):
    return jnp.dot(a, b, precision=lax.Precision.HIGHEST, preferred_element_type=jnp.float32)


def kernel(
    dx, dy,
    u_h, p_h, q_h, w_h, consts_h, out,
    u, p, q, w, consts,
    uh, xl, gbuf, grecv, ybuf, yrecv, nbuf, nrecv, summ, rin, rout, zx, ysum, yall,
    ca, cat, cb, cbt, co, cot,
    in_sem, n_send, n_recv, g_send, g_recv, c_send, c_recv,
    a_send, a_recv, b_send, b_recv, y_send, y_recv,
):
    nx, ny, nz = u.shape
    chunk = ny // dx
    mx, my = lax.axis_index("gx"), lax.axis_index("gy")
    far_first = sorted(range(1, dx), key=lambda o: abs(2 * o - dx))

    barrier = pltpu.get_barrier_semaphore()
    for off in far_first:
        pl.semaphore_signal(
            barrier, inc=1, device_id={"gx": lax.rem(mx + off, dx)}, device_id_type=MESH
        )
    for off in range(1, dy):
        pl.semaphore_signal(
            barrier, inc=1, device_id={"gy": lax.rem(my + off, dy)}, device_id_type=MESH
        )
    loads = []
    for k, (src, dst) in enumerate(
        ((q_h, q), (p_h, p), (w_h, w), (consts_h, consts), (u_h, u))
    ):
        loads.append(pltpu.make_async_copy(src, dst, in_sem.at[k]))
        loads[k].start()

    def send(src, dst, ssem, rsem, axis, peer):
        copy = pltpu.make_async_remote_copy(
            src_ref=src, dst_ref=dst, send_sem=ssem, recv_sem=rsem,
            device_id={axis: peer}, device_id_type=MESH,
        )
        copy.start()
        return copy

    for k in range(3):
        loads[k].wait()

    g = R2 * q[...]
    lane = lax.broadcasted_iota(jnp.int32, (nx, ny), 1)
    scale = 1.0 / (2.0 + 3.0 * g)
    a, b, c, d = (1.0 + g) * scale, g * scale, scale, g * scale
    stride = 1
    while stride < ny:
        ar, br, cr, dr = (pltpu.roll(m, stride, 1) for m in (a, b, c, d))
        na, nb, nc, nd = a * ar + b * cr, a * br + b * dr, c * ar + d * cr, c * br + d * dr
        scale = 1.0 / (na + nb + nc + nd)
        keep = lane >= stride
        a, b, c, d = (
            jnp.where(keep, n * scale, o)
            for n, o in ((na, a), (nb, b), (nc, c), (nd, d))
        )
        stride *= 2
    sigma = jnp.where(lane == 0, 1.0, pltpu.roll((a + b) / (c + d), 1, 1))
    ipi = 1.0 / (g + sigma)
    rho = g * ipi
    prefix = rho
    stride = 1
    while stride < ny:
        prefix = jnp.where(lane >= stride, prefix * pltpu.roll(prefix, stride, 1), prefix)
        stride *= 2
    total = prefix[:, ny - 1 :]
    before = jnp.where(lane == 0, 1.0, pltpu.roll(prefix, 1, 1))
    inverse = 1.0 / before
    row_i = lax.broadcasted_iota(jnp.int32, (ny, ny), 0)
    col_i = lax.broadcasted_iota(jnp.int32, (ny, ny), 1)
    lower = jnp.where(row_i >= col_i, 1.0, 0.0)
    upper = jnp.where(row_i <= col_i, 1.0, 0.0)
    weight = before * before * ipi
    a2 = inverse * dot(weight, lower)
    b2 = inverse * total
    cb[...] = jnp.zeros_like(cb)
    for k, m in enumerate((g, R3 * w[...], inverse, weight, a2, b2)):
        cb[k * nx : (k + 1) * nx] = m
    cbt[...] = cb[...].T
    ybuf[0] = jnp.broadcast_to(total, (nx, nz))
    ybuf[1] = jnp.broadcast_to(a2[:, 0:1], (nx, nz))
    ybuf[2] = jnp.broadcast_to((rho * sigma)[:, ny - 1 :], (nx, nz))

    gp = R1 * p[...]
    sigma = jnp.ones((1, ny), jnp.float32)
    rhos, ipis, prod = [], [], [sigma]
    for r in range(nx):
        gr = gp[r : r + 1]
        inv = 1.0 / (gr + sigma)
        rhos.append(gr * inv)
        ipis.append(inv)
        leak = rhos[r] * sigma
        sigma = 1.0 + leak
        prod.append(prod[r] * rhos[r])
    resp, tail = [None] * nx, [None] * nx
    resp[nx - 1], tail[nx - 1] = prod[nx - 1] * ipis[nx - 1], rhos[nx - 1]
    for r in range(nx - 2, -1, -1):
        resp[r] = prod[r] * ipis[r] + rhos[r] * resp[r + 1]
        tail[r] = rhos[r] * tail[r + 1]
    ca[...] = jnp.zeros_like(ca)
    for k, m in enumerate((rhos, ipis, resp, tail)):
        ca[k * nx : (k + 1) * nx] = jnp.concatenate(m, 0)
    cat[...] = ca[...].T
    nbuf[...] = jnp.zeros_like(nbuf)
    nbuf[0:1] = tail[0]
    nbuf[1:2] = resp[0]
    nbuf[2:3] = leak

    loads[3].wait()
    loads[4].wait()
    basis = consts[0:nz]
    mu = consts[nz : nz + 1]
    gbuf[0] = u[:, 0, :]
    gbuf[1] = u[:, ny - 1, :]
    gbuf[2] = q[...]
    uh[...] = dot(u[...].reshape(nx * ny, nz), basis).reshape(nx, ny, nz)

    pl.semaphore_wait(barrier, dx + dy - 2)
    g_copies = [
        send(gbuf, grecv.at[my], g_send.at[o], g_recv.at[o], "gy", lax.rem(my + o, dy))
        for o in sorted({1, dy - 1})
    ]
    n_copies = [
        send(nbuf, nrecv.at[mx], n_send.at[o], n_recv.at[o], "gx", lax.rem(mx + o, dx))
        for o in far_first
    ]
    c_copies = [
        send(ybuf, yrecv.at[my], c_send.at[o], c_recv.at[o], "gy", lax.rem(my + o, dy))
        for o in range(1, dy)
    ]
    nrecv[mx] = nbuf[...]
    yrecv[my] = ybuf[...]
    first_u = dot(gbuf[0], basis)
    for copy in g_copies:
        copy.wait()

    prev, following = lax.rem(my + dy - 1, dy), lax.rem(my + 1, dy)
    low_u = dot(grecv[prev, 1], basis)
    high_u = jnp.where(my == dy - 1, 0.0, dot(grecv[following, 0], basis))
    q_before = jnp.where(my == 0, 0.0, R2 * grecv[prev, 2][:, ny - 1 :])
    low_flux = q_before * (first_u - low_u)

    row = lax.broadcasted_iota(jnp.int32, (ny, nz), 0)
    z = None
    for r in range(nx):
        v = uh[r]
        gc = cbt[:, r : r + 1]
        wc = cbt[:, nx + r : nx + r + 1]
        after = jnp.where(row == ny - 1, high_u[r : r + 1], pltpu.roll(v, ny - 1, 0))
        flux = gc * (after - v)
        flux_before = jnp.where(row == 0, low_flux[r : r + 1], pltpu.roll(flux, 1, 0))
        h = (flux - flux_before) + (v - (wc * mu) * v)
        z = h if r == 0 else h + cat[:, r - 1 : r] * z
        xl[r] = z
    summ[0] = cat[:, nx - 1 : nx] * z
    x = z * cat[:, 2 * nx - 1 : 2 * nx]
    xl[nx - 1] = x
    for r in range(nx - 2, -1, -1):
        x = xl[r] * cat[:, nx + r : nx + r + 1] + cat[:, r : r + 1] * x
        xl[r] = x
    summ[1] = x

    def part(index):
        return pl.ds(pl.multiple_of(index * chunk, chunk), chunk)

    copies = []
    for o in far_first:
        peer = lax.rem(mx + o, dx)
        copies.append(
            send(summ.at[:, part(peer), :], rin.at[mx], a_send.at[o], a_recv.at[o], "gx", peer)
        )
    rin[mx] = summ[:, part(mx), :]

    for copy in n_copies:
        copy.wait()
    co[...] = jnp.zeros_like(co)
    tau = jnp.zeros((1, ny), jnp.float32)
    for k in range(dx):
        link, answer, leak = nrecv[k, 0:1], nrecv[k, 1:2], nrecv[k, 2:3]
        inv = 1.0 / (1.0 + answer * tau)
        co[5 * k : 5 * k + 1] = link * inv
        co[5 * k + 1 : 5 * k + 2] = link * inv * tau
        co[5 * k + 2 : 5 * k + 3] = inv
        co[5 * k + 3 : 5 * k + 4] = inv * answer
        co[5 * k + 4 : 5 * k + 5] = tau
        tau = leak + link * link * inv * tau
    cot[...] = co[...].T
    own = cot[part(mx), :]
    col = lambda k, m: own[:, 5 * k + m : 5 * k + m + 1]
    for copy in copies:
        copy.wait()
    carry = jnp.zeros((chunk, nz), jnp.float32)
    carries = []
    for k in range(dx):
        carries.append(carry)
        carry = rin[k, 0] + col(k, 0) * carry - col(k, 1) * rin[k, 1]
    carry = jnp.zeros((chunk, nz), jnp.float32)
    for k in range(dx - 1, -1, -1):
        rout[k, 1] = carry
        carry = col(k, 2) * rin[k, 1] + col(k, 3) * carries[k] + col(k, 0) * carry
        rout[k, 0] = carries[k] - col(k, 4) * carry
    copies = []
    for o in far_first:
        peer = lax.rem(mx + o, dx)
        copies.append(
            send(rout.at[peer], zx.at[:, part(mx), :], b_send.at[o], b_recv.at[o], "gx", peer)
        )
    zx[:, part(mx), :] = rout[mx]
    for copy in copies:
        copy.wait()

    for r in range(nx):
        x = (
            xl[r]
            + cat[:, 2 * nx + r : 2 * nx + r + 1] * zx[0]
            + cat[:, 3 * nx + r : 3 * nx + r + 1] * zx[1]
        )
        f = 2.0 * (x - uh[r])
        inv = cbt[:, 2 * nx + r : 2 * nx + r + 1]
        s = dot(lower, inv * f)
        ysum[0, r : r + 1, :] = s[ny - 1 :]
        y = inv * dot(upper, cbt[:, 3 * nx + r : 3 * nx + r + 1] * s)
        ysum[1, r : r + 1, :] = y[0:1]
        xl[r] = y
    copies = [
        send(ysum, yall.at[my], y_send.at[o], y_recv.at[o], "gy", lax.rem(my + o, dy))
        for o in range(1, dy)
    ]
    yall[my] = ysum[...]
    for copy in copies + c_copies:
        copy.wait()
    carry = jnp.zeros((nx, nz), jnp.float32)
    tau, carries, taus, invs = carry, [], [], []
    for k in range(dy):
        link = yrecv[k, 0]
        inv = 1.0 / (1.0 + yrecv[k, 1] * tau)
        carries.append(carry)
        taus.append(tau)
        invs.append(inv)
        carry = link * (yall[k, 0] + inv * (carry - tau * yall[k, 1]))
        tau = yrecv[k, 2] + link * link * inv * tau
    carry = jnp.zeros((nx, nz), jnp.float32)
    zeta, xi = carry, carry
    for k in range(dy - 1, -1, -1):
        xi = jnp.where(k == my, carry, xi)
        carry = invs[k] * (yall[k, 1] + yrecv[k, 1] * carries[k] + yrecv[k, 0] * carry)
        zeta = jnp.where(k == my, carries[k] - taus[k] * carry, zeta)

    for r in range(nx):
        v = (
            xl[r]
            + cbt[:, 4 * nx + r : 4 * nx + r + 1] * zeta[r : r + 1]
            + cbt[:, 5 * nx + r : 5 * nx + r + 1] * xi[r : r + 1]
        )
        v = v / (1.0 + cbt[:, nx + r : nx + r + 1] * mu)
        out[r] = u[r] + lax.dot_general(
            v, basis, (((1,), (1,)), ((), ())),
            precision=lax.Precision.HIGHEST, preferred_element_type=jnp.float32,
        )


def shards(dx, dy, u, p, q, w):
    nx, ny, nz = u.shape
    mode = np.arange(nz)
    basis = np.cos(np.pi * mode[None, :] * (mode[:, None] + 0.5) / nz) * np.sqrt(2.0 / nz)
    basis[:, 0] *= np.sqrt(0.5)
    mu = (2.0 - 2.0 * np.cos(np.pi * mode / nz))[None, :]
    consts = jnp.asarray(np.concatenate([basis, np.repeat(mu, 8, 0)]), jnp.float32)
    chunk = ny // dx
    f32 = lambda *shape: pltpu.VMEM(shape, jnp.float32)
    up = lambda n: -(-n // 128) * 128
    rows, orows = up(6 * nx), up(5 * dx)
    sems = [pltpu.SemaphoreType.DMA((5,))]
    for count in (dx, dy, dy, dx, dx, dy):
        sems += [pltpu.SemaphoreType.DMA((count,))] * 2
    return pl.pallas_call(
        functools.partial(kernel, dx, dy),
        out_shape=jax.ShapeDtypeStruct(u.shape, jnp.float32),
        in_specs=[pl.BlockSpec(memory_space=pltpu.HBM)] * 5,
        out_specs=pl.BlockSpec(memory_space=pltpu.VMEM),
        scratch_shapes=[
            f32(nx, ny, nz), f32(nx, ny), f32(nx, ny), f32(nx, ny), f32(nz + 8, nz),
            f32(nx, ny, nz), f32(nx, ny, nz), f32(3, nx, ny), f32(dy, 3, nx, ny),
            f32(3, nx, nz), f32(dy, 3, nx, nz), f32(8, ny), f32(dx, 8, ny),
            f32(2, ny, nz), f32(dx, 2, chunk, nz), f32(dx, 2, chunk, nz),
            f32(2, ny, nz), f32(2, nx, nz), f32(dy, 2, nx, nz),
            f32(rows, ny), f32(ny, rows), f32(rows, ny), f32(ny, rows),
            f32(orows, ny), f32(ny, orows),
        ] + sems,
        compiler_params=pltpu.CompilerParams(
            collective_id=0, has_side_effects=True, vmem_limit_bytes=48 * 2**20
        ),
    )(u, p, q, w, consts)


def solution(mesh):
    dx, dy = mesh.shape["gx"], mesh.shape["gy"]
    in_specs = (P("gx", "gy", None), P("gx", "gy"), P("gx", "gy"), P("gx", "gy"))
    return jax.shard_map(
        functools.partial(shards, dx, dy), mesh=mesh, in_specs=in_specs,
        out_specs=P("gx", "gy", None), check_vma=False,
    )
```

time: 34.2 us -> 31.7 us (0.927)
  local copies, waits for them, and re-layouts: 6.23 us -> 4.78 us
  Pallas kernels: 27.6 us -> 26.7 us
    unnamed x15 -> x11, local copies, waits for them, and re-layouts: 6.23 us -> 4.78 us
    pallas_call x1, Pallas kernels: 27.6 us -> 26.7 us  [shards(): pl.pallas_call(functools.partial(kernel, dx, dy), out_shape=jax.ShapeDtyp...]
where the time goes in v2:
time: 31.7 us; the launch traced here: 31.5 us
  Pallas kernels  26.7 us (84%)
  local copies, waits for them, and re-layouts  4.78 us (15%)
    pallas_call x1, Pallas kernels, shards(): pl.pallas_call(functools.partial(kernel, dx, dy), out_shape=jax.ShapeDtyp...  26.7 us
    unnamed x11, local copies, waits for them, and re-layouts  4.78 us

profile of v2, /device:TPU:0, one launch (start us, length us, event | category | flops | bytes accessed | tf_op | source)
XLA Modules:
  0.0 31.5 jit_solution(3248722776378075550)
XLA Ops:
  0.0 0.0 copy-start
  0.0 1.0 %copy-done = f32[8,128,128]{2,1,0:T(8,128)S(1)} copy-done((f32[8,128,128]{2,1,0:T(8,128)S(1)}, f32[8,128,128]{2,1,0:T(8,128)}, u32[]{:S(2)}) %copy-start) | copy-done | bytes 524312
  1.0 0.0 copy-start.1
  1.0 0.9 %copy-done.1 = f32[136,128]{1,0:T(8,128)S(1)} copy-done((f32[136,128]{1,0:T(8,128)S(1)}, f32[136,128]{1,0:T(8,128)}, u32[]{:S(2)}) %copy-start.1) | copy-done | bytes 69656
  1.9 0.0 copy-start.2
  1.9 0.7 %copy-done.2 = f32[8,128]{1,0:T(8,128)S(1)} copy-done((f32[8,128]{1,0:T(8,128)S(1)}, f32[8,128]{1,0:T(8,128)}, u32[]{:S(2)}) %copy-start.2) | copy-done | bytes 4120
  2.6 0.0 copy-start.3
  2.6 0.7 %copy-done.3 = f32[8,128]{1,0:T(8,128)S(1)} copy-done((f32[8,128]{1,0:T(8,128)S(1)}, f32[8,128]{1,0:T(8,128)}, u32[]{:S(2)}) %copy-start.3) | copy-done | bytes 4120
  3.3 0.0 copy-start.4
  3.3 0.7 %copy-done.4 = f32[8,128]{1,0:T(8,128)S(1)} copy-done((f32[8,128]{1,0:T(8,128)S(1)}, f32[8,128]{1,0:T(8,128)}, u32[]{:S(2)}) %copy-start.4) | copy-done | bytes 4120
  4.0 26.7 %shard_map.55 = f32[8,128,128]{2,1,0:T(8,128)S(1)} custom-call(f32[8,128,128]{2,1,0:T(8,128)S(1)} %copy-done, f32[8,128]{1,0:T(8,128)S(1)} %copy-done.2, f32[8,128]{1,0:T(8,128)S(1)} %copy-done.3, f32[8,128]{1,0:T(8,128)S(1)} %copy-done.4, f32[136,128]{1,0:T(8,128)S(1)} %copy-done.1), custom_call_target="tpu_custom_call" | custom-call | tf_op jit(solution)/shard_map/pallas_call | solution.py:295
  30.7 0.8 %copy.7 = f32[8,128,128]{2,1,0:T(8,128)} copy(f32[8,128,128]{2,1,0:T(8,128)S(1)} %shard_map.55) | data formatting | bytes 1048576
Async XLA Ops:
  0.0 1.0 %copy-start = (f32[8,128,128]{2,1,0:T(8,128)S(1)}, f32[8,128,128]{2,1,0:T(8,128)}, u32[]{:S(2)}) copy-start(f32[8,128,128]{2,1,0:T(8,128)} %u_h.1) | copy-start | bytes 1572868
  1.0 0.9 %copy-start.1 = (f32[136,128]{1,0:T(8,128)S(1)}, f32[136,128]{1,0:T(8,128)}, u32[]{:S(2)}) copy-start(f32[136,128]{1,0:T(8,128)} %constant.2.clone.consts_h) | copy-start | bytes 208900
  1.9 0.7 %copy-start.2 = (f32[8,128]{1,0:T(8,128)S(1)}, f32[8,128]{1,0:T(8,128)}, u32[]{:S(2)}) copy-start(f32[8,128]{1,0:T(8,128)} %p_h.1) | copy-start | bytes 12292
  2.6 0.7 %copy-start.3 = (f32[8,128]{1,0:T(8,128)S(1)}, f32[8,128]{1,0:T(8,128)}, u32[]{:S(2)}) copy-start(f32[8,128]{1,0:T(8,128)} %q_h.1) | copy-start | bytes 12292
  3.3 0.7 %copy-start.4 = (f32[8,128]{1,0:T(8,128)S(1)}, f32[8,128]{1,0:T(8,128)}, u32[]{:S(2)}) copy-start(f32[8,128]{1,0:T(8,128)} %w_h.1) | copy-start | bytes 12292

commit v3 on v2

--- a/solution.py
+++ b/solution.py
@@ -307,7 +307,7 @@
             f32(orows, ny), f32(ny, orows),
         ] + sems,
         compiler_params=pltpu.CompilerParams(
-            collective_id=0, has_side_effects=True, vmem_limit_bytes=48 * 2**20
+            collective_id=0, has_side_effects=True, vmem_limit_bytes=60 * 1024 * 2**10
         ),
     )(u, p, q, w, consts)
 

time: 31.7 us -> 29.5 us (0.931)
  local copies, waits for them, and re-layouts: 4.78 us -> 1.87 us
  Pallas kernels: 26.7 us -> 27.4 us
    unnamed x11 -> x1, local copies, waits for them, and re-layouts: 4.78 us -> 1.87 us
    pallas_call x1, Pallas kernels: 26.7 us -> 27.4 us  [shards(): pl.pallas_call(functools.partial(kernel, dx, dy), out_shape=jax.ShapeDtyp...]
where the time goes in v3:
time: 29.5 us; the launch traced here: 29.3 us
  Pallas kernels  27.4 us (93%)
  local copies, waits for them, and re-layouts  1.87 us (6%)
    pallas_call x1, Pallas kernels, shards(): pl.pallas_call(functools.partial(kernel, dx, dy), out_shape=jax.ShapeDtyp...  27.4 us
    unnamed x1, local copies, waits for them, and re-layouts  1.87 us

profile of v3, /device:TPU:0, one launch (start us, length us, event | category | flops | bytes accessed | tf_op | source)
XLA Modules:
  0.0 29.3 jit_solution(16720531745423001057)
XLA Ops:
  0.0 27.4 %shard_map.55 = f32[8,128,128]{2,1,0:T(8,128)} custom-call(f32[8,128,128]{2,1,0:T(8,128)} %u_h.1, f32[8,128]{1,0:T(8,128)} %p_h.1, f32[8,128]{1,0:T(8,128)} %q_h.1, f32[8,128]{1,0:T(8,128)} %w_h.1, f32[136,128]{1,0:T(8,128)} %constant.2.clone.consts_h), custom_call_target="tpu_custom_call" | custom-call | tf_op jit(solution)/shard_map/pallas_call | solution.py:295
  27.5 1.9 %copy.7 = f32[8,128,128]{2,1,0:T(8,128)} copy(f32[8,128,128]{2,1,0:T(8,128)} %shard_map.55) | data formatting | bytes 1048576

commit v4 on v3

--- a/solution.py
+++ b/solution.py
@@ -134,11 +134,53 @@
     gbuf[2] = q[...]
     uh[...] = dot(u[...].reshape(nx * ny, nz), basis).reshape(nx, ny, nz)
 
+    def part(index):
+        return pl.ds(pl.multiple_of(index * chunk, chunk), chunk)
+
+    def first_part(at, count, low_flux, high_u):
+        rows_at = slice(at, at + count)
+        row = lax.broadcasted_iota(jnp.int32, (count, nz), 0)
+        col = lambda k: cat[rows_at, k : k + 1]
+        z = None
+        for r in range(nx):
+            v = uh[r, rows_at]
+            gc = cbt[rows_at, r : r + 1]
+            wc = cbt[rows_at, nx + r : nx + r + 1]
+            after = jnp.where(row == count - 1, high_u[r : r + 1], pltpu.roll(v, count - 1, 0))
+            flux = gc * (after - v)
+            below = jnp.where(row == 0, low_flux[r : r + 1], pltpu.roll(flux, 1, 0))
+            h = (flux - below) + (v - (wc * mu) * v)
+            z = h if r == 0 else h + col(r - 1) * z
+            xl[r, rows_at] = z
+        summ[0, rows_at] = col(nx - 1) * z
+        x = z * col(2 * nx - 1)
+        xl[nx - 1, rows_at] = x
+        for r in range(nx - 2, -1, -1):
+            x = xl[r, rows_at] * col(nx + r) + col(r) * x
+            xl[r, rows_at] = x
+        summ[1, rows_at] = x
+
+    empty = jnp.zeros((nx, nz), jnp.float32)
+    first_part(0, ny, empty, empty)
+
     pl.semaphore_wait(barrier, dx + dy - 2)
     g_copies = [
         send(gbuf, grecv.at[my], g_send.at[o], g_recv.at[o], "gy", lax.rem(my + o, dy))
         for o in sorted({1, dy - 1})
     ]
+
+    def ends(peer, sem):
+        return pltpu.make_async_remote_copy(
+            src_ref=summ.at[:, peer * chunk : (peer + 1) * chunk, :], dst_ref=rin.at[mx],
+            send_sem=a_send.at[peer], recv_sem=a_recv.at[sem],
+            device_id={"gx": peer}, device_id_type=MESH,
+        )
+
+    middle = sorted(range(1, dx - 1), key=lambda d: abs(2 * d + 1 - dx))[::-1]
+    for peer in middle:
+        @pl.when(mx != peer)
+        def _():
+            ends(peer, mx).start()
     n_copies = [
         send(nbuf, nrecv.at[mx], n_send.at[o], n_recv.at[o], "gx", lax.rem(mx + o, dx))
         for o in far_first
@@ -157,37 +199,14 @@
     low_u = dot(grecv[prev, 1], basis)
     high_u = jnp.where(my == dy - 1, 0.0, dot(grecv[following, 0], basis))
     q_before = jnp.where(my == 0, 0.0, R2 * grecv[prev, 2][:, ny - 1 :])
-    low_flux = q_before * (first_u - low_u)
-
-    row = lax.broadcasted_iota(jnp.int32, (ny, nz), 0)
-    z = None
-    for r in range(nx):
-        v = uh[r]
-        gc = cbt[:, r : r + 1]
-        wc = cbt[:, nx + r : nx + r + 1]
-        after = jnp.where(row == ny - 1, high_u[r : r + 1], pltpu.roll(v, ny - 1, 0))
-        flux = gc * (after - v)
-        flux_before = jnp.where(row == 0, low_flux[r : r + 1], pltpu.roll(flux, 1, 0))
-        h = (flux - flux_before) + (v - (wc * mu) * v)
-        z = h if r == 0 else h + cat[:, r - 1 : r] * z
-        xl[r] = z
-    summ[0] = cat[:, nx - 1 : nx] * z
-    x = z * cat[:, 2 * nx - 1 : 2 * nx]
-    xl[nx - 1] = x
-    for r in range(nx - 2, -1, -1):
-        x = xl[r] * cat[:, nx + r : nx + r + 1] + cat[:, r : r + 1] * x
-        xl[r] = x
-    summ[1] = x
-
-    def part(index):
-        return pl.ds(pl.multiple_of(index * chunk, chunk), chunk)
-
-    copies = []
-    for o in far_first:
-        peer = lax.rem(mx + o, dx)
-        copies.append(
-            send(summ.at[:, part(peer), :], rin.at[mx], a_send.at[o], a_recv.at[o], "gx", peer)
-        )
+    first_part(0, chunk, q_before * (first_u - low_u), uh[:, chunk, :])
+    at = ny - chunk
+    gap = uh[:, at, :] - uh[:, at - 1, :]
+    first_part(at, chunk, R2 * q[:, at - 1 : at] * gap, high_u)
+    for peer in (0, dx - 1):
+        @pl.when(mx != peer)
+        def _():
+            ends(peer, mx).start()
     rin[mx] = summ[:, part(mx), :]
 
     for copy in n_copies:
@@ -206,8 +225,12 @@
     cot[...] = co[...].T
     own = cot[part(mx), :]
     col = lambda k, m: own[:, 5 * k + m : 5 * k + m + 1]
-    for copy in copies:
-        copy.wait()
+    for peer in range(dx):
+        @pl.when(mx != peer)
+        def _():
+            copy = ends(peer, peer)
+            copy.wait_send()
+            copy.wait_recv()
     carry = jnp.zeros((chunk, nz), jnp.float32)
     carries = []
     for k in range(dx):

time: 29.5 us -> 27.5 us (0.932)
  Pallas kernels: 27.4 us -> 25.5 us
    pallas_call x1, Pallas kernels: 27.4 us -> 25.5 us  [shards(): pl.pallas_call(functools.partial(kernel, dx, dy), out_shape=jax.ShapeDtyp...]
where the time goes in v4:
time: 27.5 us; the launch traced here: 27.4 us
  Pallas kernels  25.5 us (93%)
  local copies, waits for them, and re-layouts  1.87 us (7%)
    pallas_call x1, Pallas kernels, shards(): pl.pallas_call(functools.partial(kernel, dx, dy), out_shape=jax.ShapeDtyp...  25.5 us
    unnamed x1, local copies, waits for them, and re-layouts  1.87 us

profile of v4, /device:TPU:0, one launch (start us, length us, event | category | flops | bytes accessed | tf_op | source)
XLA Modules:
  0.0 27.4 jit_solution(9267380065586353620)
XLA Ops:
  0.0 25.5 %shard_map.55 = f32[8,128,128]{2,1,0:T(8,128)} custom-call(f32[8,128,128]{2,1,0:T(8,128)} %u_h.1, f32[8,128]{1,0:T(8,128)} %p_h.1, f32[8,128]{1,0:T(8,128)} %q_h.1, f32[8,128]{1,0:T(8,128)} %w_h.1, f32[136,128]{1,0:T(8,128)} %constant.2.clone.consts_h), custom_call_target="tpu_custom_call" | custom-call | tf_op jit(solution)/shard_map/pallas_call | solution.py:318
  25.5 1.9 %copy.7 = f32[8,128,128]{2,1,0:T(8,128)} copy(f32[8,128,128]{2,1,0:T(8,128)} %shard_map.55) | data formatting | bytes 1048576
